TPU v7x, 256 devices: a whole 4x4x8 slice. The times are simulated.
256 devices in a mesh: dp: 4 (over z_hi), row: 16 (over y, x), col: 4 (over z_lo, core).
Axes of the slice: x: 4, y: 4, z: 8 (z_hi: 4, z_lo: 2; z = z_hi * 2 + z_lo), core: 2. Of those that a mesh axis runs over, the one named last changes fastest.
Arguments:
- grad_partials: float32 [4, 4, 2048, 16384], P('dp', None, 'row', 'col'), may hold values from -300 to 300, as said below
- master_weights: float32 [8192, 16384], P(('dp', 'row'), 'col'), may hold values from -1.5 to 1.5
- row_moment: float32 [8192], P(('dp', 'row')), may hold values from 0.3 to 30
- col_moment: float32 [16384], P('col'), may hold values from 0.003 to 0.3
Outputs:
- new_master: float32 [8192, 16384], P(('dp', 'row'), 'col')
- new_row_moment: float32 [8192], P(('dp', 'row'))
- new_col_moment: float32 [16384], P('col')
- compute_weights: bfloat16 [4, 2048, 16384], P(None, 'row', 'col')
- rms_update: float32 [], replicated
Inputs may be any that keep to these rules, and one draw needn't show every extreme that they name: `grad_partials`: finite gradient partials.
All inputs are finite; a program needn't handle non-finite values.
Results may differ from a plain program's by a relative error of at most 0.0004.
Values may be sent and summed in bfloat16 or wider, within the bound.
A program may use at most 128 MiB of HBM per device.

v0:
```python
import jax
import jax.numpy as jnp
from jax import lax
from jax.sharding import PartitionSpec as P

decay_rate = 0.9
step_rate = 0.05
tiny_value = 1e-30


def local(grad_partials, master_weights, row_moment, col_moment):
    local_grads = grad_partials[0]
    row_dev = master_weights.shape[0]
    col_dev = master_weights.shape[1]
    groups = lax.axis_size("dp")
    all_rows = row_dev * groups * lax.axis_size("row")
    full_width = col_dev * lax.axis_size("col")
    summed = lax.psum_scatter(local_grads, "dp", scatter_dimension=0, tiled=True)
    gradient = summed.reshape(row_dev, col_dev)
    weights_all, moments_all = (master_weights, row_moment)
    squared = gradient * gradient
    row_totals = lax.psum(jnp.sum(squared, axis=1), "col")
    local_cols = jnp.sum(squared, axis=0)
    row_mean = row_totals / full_width + tiny_value
    new_rows = decay_rate * moments_all + (1.0 - decay_rate) * row_mean
    rows_sum = jnp.sum(new_rows)
    col_totals, moment_sum = lax.psum((local_cols, rows_sum), ("dp", "row"))
    col_mean = col_totals / all_rows + tiny_value
    new_cols = decay_rate * col_moment + (1.0 - decay_rate) * col_mean
    scale_mean = moment_sum / all_rows
    update = gradient * lax.rsqrt(new_rows[:, None] * new_cols[None, :] / scale_mean)
    update_local = jnp.sum(update * update)
    update_sum = lax.psum(update_local, ("dp", "row", "col"))
    entry_count = float(all_rows * full_width)
    rms_update = jnp.sqrt(update_sum / entry_count)
    new_weights = weights_all - step_rate * update / jnp.maximum(1.0, rms_update)
    copies = lax.all_gather(new_weights.astype(jnp.bfloat16)[None], "dp", axis=0, tiled=True)
    return (new_weights, new_rows, new_cols, copies, rms_update)


def solution(mesh):
    return jax.shard_map(
        local,
        mesh=mesh,
        in_specs=(P("dp", None, "row", "col"), P(("dp", "row"), "col"), P(("dp", "row")), P("col")),
        out_specs=(P(("dp", "row"), "col"), P(("dp", "row")), P("col"), P(None, "row", "col"), P()),
        check_vma=False,
    )
```

profile of v0, /device:TPU:1, one launch (start us, length us, event | category | flops | bytes accessed | tf_op | source)
XLA Modules:
  0.0 718.2 jit_solution(2824089146126804063)
XLA Ops:
  7.2 0.0 reduce-scatter.2.cloned.1.call-start
  7.2 0.7 reduce-scatter.2.cloned.1.call-update
  7.9 0.0 copy-start.4
  7.9 0.0 copy-start.2
  7.9 0.0 all-gather.3.cloned.1.call-start
  8.0 158.5 %reduce-scatter.2.cloned.1.call-done = f32[1,128,4096]{2,1,0:T(8,128)} async-done(((f32[4,128,4096]{2,1,0:T(8,128)}), f32[1,128,4096]{2,1,0:T(8,128)}) %reduce-scatter.2.cloned.1.call-update) | async-done | bytes 2097168 | tf_op jit(solution)/shard_map/reduce_scatter | solution.py:18
  166.4 0.0 copy-start
  166.4 2.0 fusion
  168.5 5.6 psum.28
  174.1 0.0 copy-done.4
  174.1 0.6 fusion.3
  174.7 0.0 copy-start.3
  174.7 323.9 %all-reduce = (f32[]{:T(128)}, f32[4096]{0:T(1024)S(1)}) all-reduce(f32[]{:T(128)} %get-tuple-element.11, f32[4096]{0:T(1024)S(1)} %get-tuple-element.5), channel_id=1, replica_groups=mesh['dp'=4,'row'=16,'col'=4] {'dp','row'}, use_global_device_ids=true, to_apply=%region_6.0 | all-reduce | flops 4097 | bytes 32776 | tf_op jit(solution)/shard_map/psum | solution.py:27
  499.3 0.0 copy-done.2
  499.3 0.0 copy-start.1
  499.3 0.0 copy-done
  499.3 1.2 multiply_reduce_fusion
  500.5 126.7 %psum.31 = f32[]{:T(128)} all-reduce(f32[]{:T(128)} %multiply_reduce_fusion), channel_id=1, replica_groups=mesh['dp'=4,'row'=16,'col'=4] {'dp','row','col'}, use_global_device_ids=true, to_apply=%region_8.0 | all-reduce | flops 1 | bytes 8 | tf_op jit(solution)/shard_map/psum | solution.py:33
  627.9 3.9 fusion.2
  631.8 0.0 copy-done.3
  631.8 0.0 copy-done.1
  631.8 0.0 all-gather.3.cloned.1.call-update
  631.8 73.7 %all-gather.3.cloned.1.call-done = bf16[512,4096]{1,0:T(8,128)(2,1)} async-done(((bf16[128,4096]{1,0:T(8,128)(2,1)}), bf16[512,4096]{1,0:T(8,128)(2,1)}) %all-gather.3.cloned.1.call-update) | async-done | bytes 4194320 | tf_op jit(solution)/shard_map/all_gather | solution.py:37
  705.5 4.7 copy.10
  (1 shorter events, 0.0 us)
Async XLA Ops:
  7.2 159.3 %reduce-scatter.2.cloned.1.call-start = ((), (), s32[]{:S(2)}) async-start(), calls=%async_computation.1 | async-start | bytes 10485760 | tf_op jit(solution)/shard_map/reduce_scatter | solution.py:18
  7.9 166.2 %copy-start.4 = (f32[128]{0:T(128)S(1)}, f32[128]{0:T(128)}, u32[]{:S(2)}) copy-start(f32[128]{0:T(128)} %param.6) | copy-start | bytes 1540
  7.9 491.3 %copy-start.2 = (f32[4096]{0:T(1024)S(1)}, f32[4096]{0:T(1024)}, u32[]{:S(2)}) copy-start(f32[4096]{0:T(1024)} %param.7) | copy-start | bytes 49156
  7.9 697.6 %all-gather.3.cloned.1.call-start = ((), (), s32[]{:S(2)}) async-start(), calls=%async_computation.2 | async-start | bytes 5242880 | tf_op jit(solution)/shard_map/all_gather | solution.py:37
  166.4 332.9 %copy-start = (f32[1,128,4096]{2,1,0:T(8,128)S(1)}, f32[1,128,4096]{2,1,0:T(8,128)}, u32[]{:S(2)}) copy-start(f32[1,128,4096]{2,1,0:T(8,128)} %reduce-scatter.2.cloned.1.call-done) | copy-start | bytes 6291460
  174.7 457.1 %copy-start.3 = (f32[128]{0:T(128)}, f32[128]{0:T(128)S(1)}, u32[]{:S(2)}) copy-start(f32[128]{0:T(128)S(1)} %get-tuple-element.19) | copy-start | bytes 1540
  499.3 132.5 %copy-start.1 = (f32[4096]{0:T(1024)}, f32[4096]{0:T(1024)S(1)}, u32[]{:S(2)}) copy-start(f32[4096]{0:T(1024)S(1)} %multiply_add_fusion) | copy-start | bytes 49156
Sparse Core Ops, SparseCore 0:
  10.6 155.7 reduce-scatter.1
  632.0 73.5 all-gather.2
where the time goes:
time: 727 us; the launch traced here: 718 us
  blocking collectives  456 us (63%)
  waiting for transfers between devices  233 us (32%)
  between operations  16.6 us (2%)
  other arithmetic  7.76 us (1%)
    psum x1, blocking collectives, local(): col_totals, moment_sum = lax.psum((local_cols, rows_sum), ('dp', 'row'))  324 us
    reduce_scatter x1, waiting for transfers between devices, local(): lax.psum_scatter(local_grads, 'dp', scatter_dimension=0, tiled=True)  158 us
    psum x1, blocking collectives, local(): update_sum = lax.psum(update_local, ('dp', 'row', 'col'))  127 us
    all_gather x1, waiting for transfers between devices, local(): lax.all_gather(new_weights.astype(jnp.bfloat16)[None], 'dp', axis=0, tile...  73.7 us
  transfers between devices with their start and end apart: 2, of which 2 were waited for; matrix products, arithmetic and copies ran while one was open for 0% of the time, Pallas kernels for 0%

commit v1 on v0

v1 whole, which is shorter than its diff:
```python
import functools

import jax
import jax.numpy as jnp
from jax import lax
from jax.experimental import pallas as pl
from jax.experimental.pallas import tpu as pltpu
from jax.sharding import PartitionSpec as P

decay_rate = 0.9
step_rate = 0.05
tiny_value = 1e-30

MESH = pl.DeviceIdType.MESH
LANES = 128
X_SIZE = 4
RS_ROWS = 8
AG_ROWS = 16


def kernel(all_rows, full_width, grads, master, row_mom, col_mom,
           new_master, new_rows, new_cols, copies, rms_out,
           opp_l, opp_r, add_r, add_l, own_l, own_r, mine, mast, wb,
           row_part, col_part, inv_cols, inv_rows, x_buf, y_buf, d_buf, r_buf,
           s_bufs, load_sem, rs_send, rs_recv, st_send, st_recv, ag_send, ag_recv, out_sem):
    dp, row, col = lax.axis_index("dp"), lax.axis_index("row"), lax.axis_index("col")
    y, x = row // X_SIZE, row % X_SIZE
    right, left, far = (dp + 1) % 4, (dp + 3) % 4, (dp + 2) % 4
    rows, width = mine.shape
    half = rows // 2
    rs_n = half // RS_ROWS
    groups = width // LANES

    def x_peer(j):
        return {"row": y * X_SIZE + (x + j) % X_SIZE}

    def y_peer(j):
        return {"row": ((y + j) % 4) * X_SIZE + x}

    def d_peer(j):
        return {"dp": (dp + j) % 4}

    def c_peer(j):
        return {"col": (col + j) % 4}

    loads = [
        pltpu.make_async_copy(grads.at[0, right, pl.ds(0, half)], add_r, load_sem.at[0]),
        pltpu.make_async_copy(grads.at[0, left, pl.ds(half, half)], add_l, load_sem.at[1]),
        pltpu.make_async_copy(grads.at[0, dp], mine, load_sem.at[2]),
        pltpu.make_async_copy(master, mast, load_sem.at[3]),
    ]
    for load in loads:
        load.start()

    barrier = pltpu.get_barrier_semaphore()
    for peer in (x_peer, y_peer, d_peer, c_peer):
        for j in (1, 2, 3):
            pl.semaphore_signal(barrier, inc=1, device_id=peer(j), device_id_type=MESH)
    pl.semaphore_wait(barrier, 12)

    def rs_copy(way, phase, k):
        to = right if way == 0 else left
        at = pl.multiple_of(k * RS_ROWS, RS_ROWS)
        low, high = pl.ds(at, RS_ROWS), pl.ds(pl.multiple_of(half + at, RS_ROWS), RS_ROWS)
        near, other = (low, high) if way == 0 else (high, low)
        opp, own, add = (opp_l, own_l, add_r) if way == 0 else (opp_r, own_r, add_l)
        if phase == 0:
            src, dst = grads.at[0, far, near], opp.at[low]
        elif phase == 1:
            src, dst = grads.at[0, to, other], own.at[other]
        else:
            src, dst = add.at[low], own.at[near]
        return pltpu.make_async_remote_copy(
            src_ref=src, dst_ref=dst, send_sem=rs_send.at[way, phase, k], recv_sem=rs_recv.at[way, phase, k],
            device_id={"dp": to}, device_id_type=MESH)

    @pl.loop(0, rs_n)
    def _(k):
        rs_copy(0, 0, k).start()
        rs_copy(1, 0, k).start()

    loads[0].wait()
    loads[1].wait()

    @pl.loop(0, rs_n)
    def _(k):
        at = pl.ds(pl.multiple_of(k * RS_ROWS, RS_ROWS), RS_ROWS)
        rs_copy(0, 1, k).start()
        rs_copy(1, 1, k).start()
        rs_copy(0, 0, k).wait_recv()
        add_r[at] = add_r[at] + opp_l[at]
        rs_copy(0, 2, k).start()
        rs_copy(1, 0, k).wait_recv()
        add_l[at] = add_l[at] + opp_r[at]
        rs_copy(1, 2, k).start()

    loads[2].wait()
    col_part[...] = jnp.zeros_like(col_part)

    def take(at):
        total = jnp.zeros((RS_ROWS, LANES), jnp.float32)
        for c in range(groups):
            lanes = pl.ds(c * LANES, LANES)
            g = mine[at, lanes] + own_l[at, lanes] + own_r[at, lanes]
            mine[at, lanes] = g
            square = g * g
            total = total + square
            col_part[:, lanes] = col_part[:, lanes] + square
        row_part[at] = total

    @pl.loop(0, rs_n)
    def _(k):
        at = k * RS_ROWS
        rs_copy(1, 1, k).wait_recv()
        rs_copy(0, 2, k).wait_recv()
        take(pl.ds(pl.multiple_of(at, RS_ROWS), RS_ROWS))
        rs_copy(0, 1, k).wait_recv()
        rs_copy(1, 2, k).wait_recv()
        take(pl.ds(pl.multiple_of(half + at, RS_ROWS), RS_ROWS))

    def exchange(stage, buf, me, peer):
        def one(j):
            return pltpu.make_async_remote_copy(
                src_ref=buf.at[me], dst_ref=buf.at[me], send_sem=st_send.at[stage, j - 1],
                recv_sem=st_recv.at[stage, j - 1], device_id=peer(j), device_id_type=MESH)
        for j in (1, 2, 3):
            one(j).start()
        return one

    def finish(one):
        for j in (1, 2, 3):
            one(j).wait_recv()

    def total_of(buf):
        return (buf[0] + buf[1]) + (buf[2] + buf[3])

    x_buf[x] = jnp.sum(col_part[...], axis=0, keepdims=True)
    x_copy = exchange(0, x_buf, x, x_peer)
    eye = lax.broadcasted_iota(jnp.int32, (rows, LANES), 0) == lax.broadcasted_iota(jnp.int32, (rows, LANES), 1)
    row_sums = jnp.sum(row_part[...], axis=1, keepdims=True)
    r_buf[col] = jnp.sum(jnp.where(eye, row_sums, 0.0), axis=0, keepdims=True)
    r_copy = exchange(1, r_buf, col, c_peer)
    finish(x_copy)
    y_buf[y] = total_of(x_buf)
    y_copy = exchange(2, y_buf, y, y_peer)
    finish(r_copy)
    row_mean = total_of(r_buf) / full_width + tiny_value
    next_rows = decay_rate * row_mom[...] + (1.0 - decay_rate) * row_mean
    new_rows[...] = next_rows
    rows_down = jnp.sum(jnp.where(eye, next_rows, 0.0), axis=1, keepdims=True)
    inv_rows[...] = jnp.broadcast_to(1.0 / rows_down, inv_rows.shape)
    finish(y_copy)
    d_buf[dp] = total_of(y_buf)
    d_copy = exchange(3, d_buf, dp, d_peer)
    finish(d_copy)
    col_mean = total_of(d_buf) / all_rows + tiny_value
    next_cols = decay_rate * col_mom[...] + (1.0 - decay_rate) * col_mean
    new_cols[...] = next_cols
    inv_cols[...] = jnp.broadcast_to(1.0 / next_cols, inv_cols.shape)

    def add_squares(k, acc):
        at = pl.ds(pl.multiple_of(k * 8, 8), 8)
        part = jnp.zeros((8, LANES), jnp.float32)
        for c in range(groups):
            lanes = pl.ds(c * LANES, LANES)
            g = mine[at, lanes]
            part = part + g * g * inv_cols[:, lanes]
        return acc + part * inv_rows[at]

    squares = lax.fori_loop(0, rows // 8, add_squares, jnp.zeros((8, LANES), jnp.float32))

    first = lax.broadcasted_iota(jnp.int32, (8, LANES), 0) == 0
    s_bufs[0, col, 0] = squares
    s_bufs[0, col, 1] = jnp.where(first, jnp.broadcast_to(next_rows, (8, LANES)), 0.0)
    for stage, (me, peer) in enumerate(((col, c_peer), (x, x_peer), (y, y_peer), (dp, d_peer))):
        finish(exchange(4 + stage, s_bufs.at[stage], me, peer))
        both = total_of(s_bufs.at[stage])
        if stage < 3:
            s_bufs[stage + 1, (x, y, dp)[stage]] = both
    scale_mean = jnp.sum(both[1], axis=(0, 1), keepdims=True) / (4.0 * all_rows)
    update_sum = jnp.sum(both[0], axis=(0, 1), keepdims=True) * scale_mean
    rms_update = jnp.sqrt(update_sum / (float(all_rows) * float(full_width)))
    rms_out[...] = rms_update
    factor = step_rate * jnp.sqrt(scale_mean) / jnp.maximum(1.0, rms_update)
    inv_cols[...] = jnp.sqrt(inv_cols[...]) * factor
    inv_rows[...] = jnp.sqrt(inv_rows[...])
    loads[3].wait()

    ag_n = rows // AG_ROWS

    def ag_copy(way, k, passed):
        to = right if way == 0 else left
        at = pl.ds(pl.multiple_of(k * AG_ROWS, AG_ROWS), AG_ROWS)
        if passed:
            slot = left if way == 0 else right
            src, sem = copies.at[slot, at], ag_n + k % (ag_n // 2)
        else:
            slot, src, sem = dp, wb.at[at], k
        return pltpu.make_async_remote_copy(
            src_ref=src, dst_ref=copies.at[slot, at], send_sem=ag_send.at[way, sem], recv_sem=ag_recv.at[way, sem],
            device_id={"dp": to}, device_id_type=MESH)

    def ag_arrived(way, k, passed):
        return ag_copy(way, k, passed)

    def out_copies(k):
        at = pl.ds(pl.multiple_of(k * AG_ROWS, AG_ROWS), AG_ROWS)
        return (pltpu.make_async_copy(mast.at[at], new_master.at[at], out_sem.at[0, k]),
                pltpu.make_async_copy(wb.at[at], copies.at[dp, at], out_sem.at[1, k]))

    def give(k):
        base = pl.multiple_of(k * AG_ROWS, AG_ROWS)
        at = pl.ds(base, AG_ROWS)
        scale = inv_rows[at]
        for c in range(groups):
            lanes = pl.ds(c * LANES, LANES)
            across = inv_cols[:, lanes]
            across = jnp.concatenate([across, across], axis=0)
            w = mast[at, lanes] - mine[at, lanes] * scale * across
            mast[at, lanes] = w
            wb[at, lanes] = w.astype(jnp.bfloat16)

    ag_half = ag_n // 2

    @pl.loop(0, ag_half)
    def _(k):
        give(k)
        ag_copy(0, k, False).start()
        give(k + ag_half)
        ag_copy(1, k + ag_half, False).start()

    @pl.loop(0, ag_half)
    def _(k):
        ag_copy(0, k + ag_half, False).start()
        ag_copy(1, k, False).start()
        for o in (k, k + ag_half):
            for c in out_copies(o):
                c.start()

    @pl.loop(0, ag_half)
    def _(k):
        ag_copy(0, k, False).wait_recv()
        ag_copy(0, k, True).start()
        ag_copy(1, k + ag_half, False).wait_recv()
        ag_copy(1, k + ag_half, True).start()

    @pl.loop(0, ag_half)
    def _(k):
        ag_copy(0, k + ag_half, False).wait_recv()
        ag_copy(1, k, False).wait_recv()
        ag_copy(0, k, True).wait_recv()
        ag_copy(1, k + ag_half, True).wait_recv()
        ag_copy(0, k, True).wait_send()
        ag_copy(1, k + ag_half, True).wait_send()
        for o in (k, k + ag_half):
            ag_copy(0, o, False).wait_send()
            ag_copy(1, o, False).wait_send()
            for c in out_copies(o):
                c.wait()

    @pl.loop(0, rs_n)
    def _(k):
        for way in (0, 1):
            for phase in (0, 1, 2):
                rs_copy(way, phase, k).wait_send()

    stages = ((x_buf, x, x_peer), (r_buf, col, c_peer), (y_buf, y, y_peer), (d_buf, dp, d_peer),
              (s_bufs.at[0], col, c_peer), (s_bufs.at[1], x, x_peer), (s_bufs.at[2], y, y_peer), (s_bufs.at[3], dp, d_peer))
    for stage, (buf, me, peer) in enumerate(stages):
        for j in (1, 2, 3):
            pltpu.make_async_remote_copy(
                src_ref=buf.at[me], dst_ref=buf.at[me], send_sem=st_send.at[stage, j - 1],
                recv_sem=st_recv.at[stage, j - 1], device_id=peer(j), device_id_type=MESH).wait_send()


def local(grad_partials, master_weights, row_moment, col_moment):
    rows, width = master_weights.shape
    all_rows = rows * lax.axis_size("dp") * lax.axis_size("row")
    full_width = width * lax.axis_size("col")
    half = rows // 2
    rs_n, ag_n = half // RS_ROWS, rows // AG_ROWS
    f32 = jnp.float32
    anywhere = pl.BlockSpec(memory_space=pl.ANY)
    vmem = pl.BlockSpec(memory_space=pltpu.VMEM)
    new_master, new_rows, new_cols, copies, rms = pl.pallas_call(
        functools.partial(kernel, all_rows, full_width),
        out_shape=(
            jax.ShapeDtypeStruct((rows, width), f32),
            jax.ShapeDtypeStruct((1, rows), f32),
            jax.ShapeDtypeStruct((1, width), f32),
            jax.ShapeDtypeStruct((4, rows, width), jnp.bfloat16),
            jax.ShapeDtypeStruct((1, 1), f32),
        ),
        in_specs=[anywhere, anywhere, vmem, vmem],
        out_specs=(anywhere, vmem, vmem, anywhere, vmem),
        scratch_shapes=[
            pltpu.VMEM((half, width), f32), pltpu.VMEM((half, width), f32),
            pltpu.VMEM((half, width), f32), pltpu.VMEM((half, width), f32),
            pltpu.VMEM((rows, width), f32), pltpu.VMEM((rows, width), f32),
            pltpu.VMEM((rows, width), f32), pltpu.VMEM((rows, width), f32),
            pltpu.VMEM((rows, width), jnp.bfloat16),
            pltpu.VMEM((rows, LANES), f32), pltpu.VMEM((8, width), f32), pltpu.VMEM((8, width), f32),
            pltpu.VMEM((rows, LANES), f32),
            pltpu.VMEM((4, 1, width), f32), pltpu.VMEM((4, 1, width), f32), pltpu.VMEM((4, 1, width), f32),
            pltpu.VMEM((4, 1, rows), f32),
            pltpu.VMEM((4, 4, 2, 8, LANES), f32),
            pltpu.SemaphoreType.DMA((4,)),
            pltpu.SemaphoreType.DMA((2, 3, rs_n)), pltpu.SemaphoreType.DMA((2, 3, rs_n)),
            pltpu.SemaphoreType.DMA((8, 3)), pltpu.SemaphoreType.DMA((8, 3)),
            pltpu.SemaphoreType.DMA((2, ag_n + ag_n // 2)), pltpu.SemaphoreType.DMA((2, ag_n + ag_n // 2)),
            pltpu.SemaphoreType.DMA((2, ag_n)),
        ],
        compiler_params=pltpu.CompilerParams(
            collective_id=0, has_side_effects=True, vmem_limit_bytes=40 * 1024 * 1024),
        cost_estimate=pl.CostEstimate(flops=10 * rows * width, bytes_accessed=40 * rows * width, transcendentals=0),
        name="adafactor",
    )(grad_partials, master_weights, row_moment.reshape(1, rows), col_moment.reshape(1, width))
    return (new_master, new_rows.reshape(rows), new_cols.reshape(width), copies, rms.reshape(()))


def solution(mesh):
    return jax.shard_map(
        local,
        mesh=mesh,
        in_specs=(P("dp", None, "row", "col"), P(("dp", "row"), "col"), P(("dp", "row")), P("col")),
        out_specs=(P(("dp", "row"), "col"), P(("dp", "row")), P("col"), P(None, "row", "col"), P()),
        check_vma=False,
    )
```

time: 727 us -> 253 us (0.35); the launches traced: 718 us -> 253 us
  blocking collectives: 456 us -> 0 us
  Pallas kernels: 0 us -> 243 us
  waiting for transfers between devices: 233 us -> 0 us
  between operations: 16.6 us -> 2.39 us
  other arithmetic: 7.76 us -> 0 us
    psum x3 -> x0, blocking collectives: 456 us -> none  [the longest x1 324 us: local(): col_totals, moment_sum = lax.psum((local_cols, rows_sum), ('dp', 'row'))]
    pallas_call x0 -> x1, Pallas kernels: none -> 243 us  [local(): pl.pallas_call(functools.partial(kernel, all_rows, full_width), out_shape...]
    reduce_scatter x1 -> x0, waiting for transfers between devices: 158 us -> none  [local(): lax.psum_scatter(local_grads, 'dp', scatter_dimension=0, tiled=True)]
    all_gather x1 -> x0, waiting for transfers between devices: 73.7 us -> none  [local(): lax.all_gather(new_weights.astype(jnp.bfloat16)[None], 'dp', axis=0, tile...]
  transfers between devices with their start and end apart: 2 -> 0, of which waited for: 2 -> 0; matrix products, arithmetic and copies ran while one was open for 0% -> 0% of each run, Pallas kernels for 0% -> 0%
where the time goes in v1:
time: 253 us
  Pallas kernels  243 us (96%)
  local copies, waits for them, and re-layouts  7.41 us (3%)
    pallas_call x1, Pallas kernels, local(): pl.pallas_call(functools.partial(kernel, all_rows, full_width), out_shape...  243 us
    unnamed x10, local copies, waits for them, and re-layouts  7.41 us

profile of v1, /device:TPU:1, one launch (start us, length us, event | category | flops | bytes accessed | tf_op | source)
XLA Modules:
  0.0 253.0 jit_solution(16962962226181700299)
XLA Ops:
  0.6 0.0 copy-start
  0.6 1.6 copy-done
  2.2 0.0 copy-start.1
  2.2 0.7 copy-done.1
  2.9 0.0 copy-start.2
  2.9 0.7 copy-done.2
  3.6 243.2 %adafactor.1 = (f32[128,4096]{1,0:T(8,128)S(1)}, f32[1,128]{1,0:T(1,128)S(1)}, f32[1,4096]{1,0:T(1,128)S(1)}, bf16[4,128,4096]{2,1,0:T(8,128)(2,1)S(1)}, f32[1,1]{1,0:T(1,128)}) custom-call(f32[1,4,128,4096]{3,2,1,0:T(8,128)} %grads.1, f32[128,4096]{1,0:T(8,128)S(1)} %copy-done, f32[1,128]{1,0:T(1,128)S(1)} %bitcast.7, f32[1,4096]{1,0:T(1,128)S(1)} %bitcast.5), custom_call_target="tpu_custom_call" | custom-call | flops 5242880 | bytes 20971520 | tf_op jit(solution)/shard_map/adafactor/pallas_call | solution.py:285
  246.8 1.3 copy.14
  248.1 0.5 copy.15
  248.6 0.6 copy.16
  249.2 2.0 copy.17
Async XLA Ops:
  0.6 1.6 copy-start
  2.2 0.7 copy-start.1
  2.9 0.7 copy-start.2

commit v2 on v0

v2 whole, which is shorter than its diff:
```python
import functools

import jax
import jax.numpy as jnp
from jax import lax
from jax.experimental import pallas as pl
from jax.experimental.pallas import tpu as pltpu
from jax.sharding import PartitionSpec as P

decay_rate = 0.9
step_rate = 0.05
tiny_value = 1e-30

MESH = pl.DeviceIdType.MESH
LANES = 128
CHUNK = 256
LATE = 1280
AHEAD = 1
AG_ROWS = 16


def kernel(all_rows, full_width, grads, master, row_mom_hbm, col_mom_hbm,
           new_master, new_rows, new_cols, copies, rms_out,
           opp_l, opp_r, add_r, add_l, own_l, own_r, mine, mast, row_mom, col_mom,
           row_part, w_part, col_part, inv_cols, inv_rows, x_buf, y_buf, d_buf, r_buf, f_buf, g_buf,
           load_sem, rs_send, rs_recv, st_send, st_recv, ag_send, ag_recv, ready):
    dp, row, col = lax.axis_index("dp"), lax.axis_index("row"), lax.axis_index("col")
    y, x = row // 4, row % 4
    right, left, far = (dp + 1) % 4, (dp + 3) % 4, (dp + 2) % 4
    rows, width = mine.shape
    half = rows // 2
    strips = rows // 8
    rs_n = width // CHUNK
    early = width - LATE
    early_n = early // CHUNK

    def x_peer(j):
        return {"row": y * 4 + (x + j) % 4}

    def y_peer(j):
        return {"row": ((y + j) % 4) * 4 + x}

    def d_peer(j):
        return {"dp": (dp + j) % 4}

    def c_peer(j):
        return {"col": (col + j) % 4}

    def row_peer(j):
        return {"row": (row + j) % 16}

    def z_peer(j):
        to = (dp * 4 + col + j) % 16
        return {"dp": to // 4, "col": to % 4}

    def signal(sem, peer):
        pl.semaphore_signal(sem, inc=1, device_id=peer, device_id_type=MESH)

    near = [d_peer(1), d_peer(3), x_peer(1), x_peer(3), y_peer(1), y_peer(3), c_peer(1), c_peer(2), c_peer(3)]
    barrier = pltpu.get_barrier_semaphore()
    for peer in near:
        signal(barrier, peer)

    loads = [
        pltpu.make_async_copy(grads.at[0, right, pl.ds(0, half)], add_r, load_sem.at[0]),
        pltpu.make_async_copy(grads.at[0, left, pl.ds(half, half)], add_l, load_sem.at[1]),
        pltpu.make_async_copy(grads.at[0, dp], mine, load_sem.at[2]),
        pltpu.make_async_copy(row_mom_hbm, row_mom, load_sem.at[3]),
        pltpu.make_async_copy(col_mom_hbm, col_mom, load_sem.at[4]),
        pltpu.make_async_copy(master, mast, load_sem.at[5]),
    ]
    for load in loads:
        load.start()
    pl.semaphore_wait(barrier, len(near))

    def rs_copy(way, phase, k):
        to = right if way == 0 else left
        at = pl.ds(pl.multiple_of(k * CHUNK, CHUNK), CHUNK)
        low, high = pl.ds(0, half), pl.ds(half, half)
        mid, other = (low, high) if way == 0 else (high, low)
        opp, own, add = (opp_l, own_l, add_r) if way == 0 else (opp_r, own_r, add_l)
        if phase == 0:
            src, dst = grads.at[0, far, mid, at], opp.at[:, at]
        elif phase == 1:
            src, dst = grads.at[0, to, other, at], own.at[other, at]
        else:
            src, dst = add.at[:, at], own.at[mid, at]
        return pltpu.make_async_remote_copy(
            src_ref=src, dst_ref=dst, send_sem=rs_send.at[way, phase], recv_sem=rs_recv.at[way, min(phase, 1), k],
            device_id={"dp": to}, device_id_type=MESH)

    for k in range(AHEAD):
        rs_copy(0, 0, k).start()
        rs_copy(1, 0, k).start()

    for peer in near:
        signal(ready.at[0], peer)
    row_part[...] = jnp.zeros_like(row_part)
    loads[0].wait()
    loads[1].wait()
    loads[2].wait()
    pl.semaphore_wait(ready.at[0], len(near))
    for j in (1, 2, 3):
        signal(ready.at[1], y_peer(j))
        signal(ready.at[1], d_peer(j))

    def add_strips(add, opp, k):
        at = pl.ds(pl.multiple_of(k * CHUNK, CHUNK), CHUNK)
        for r in range(half // 8):
            down = pl.ds(8 * r, 8)
            add[down, at] = add[down, at] + opp[down, at]

    def take(k):
        at = pl.ds(pl.multiple_of(k * CHUNK, CHUNK), CHUNK)
        for way, own in enumerate((own_l, own_r)):
            pltpu.make_async_copy(own.at[:, at], own.at[:, at], rs_recv.at[way, 1, k]).wait()
        cols = jnp.zeros((8, CHUNK), jnp.float32)
        for r in range(strips):
            down = pl.ds(8 * r, 8)
            g = mine[down, at] + own_l[down, at] + own_r[down, at]
            mine[down, at] = g
            square = g * g
            cols = cols + square
            across = square[:, :LANES]
            for c in range(1, CHUNK // LANES):
                across = across + square[:, c * LANES:(c + 1) * LANES]
            row_part[down] = row_part[down] + across
        col_part[:, at] = jnp.sum(cols, axis=0, keepdims=True)

    def step(k, more=True):
        if more:
            rs_copy(0, 0, k + AHEAD).start()
            rs_copy(1, 0, k + AHEAD).start()
        rs_copy(0, 1, k).start()
        rs_copy(1, 1, k).start()
        rs_copy(0, 0, k).wait_recv()
        add_strips(add_r, opp_l, k)
        rs_copy(0, 2, k).start()
        rs_copy(1, 0, k).wait_recv()
        add_strips(add_l, opp_r, k)
        rs_copy(1, 2, k).start()

    @pl.loop(0, early_n + 2)
    def _(k):
        step(k)

        @pl.when(k >= 2)
        def _():
            take(k - 2)

    pl.semaphore_wait(ready.at[1], 6)

    def stage_copy(stage, buf, me, peer, j):
        return pltpu.make_async_remote_copy(
            src_ref=buf.at[me], dst_ref=buf.at[me], send_sem=st_send.at[stage],
            recv_sem=st_recv.at[stage], device_id=peer(j), device_id_type=MESH)

    stages = ((x_buf, x, x_peer), (y_buf, y, y_peer), (d_buf, dp, d_peer), (r_buf, col, c_peer),
              (f_buf, row, row_peer), (g_buf, dp * 4 + col, z_peer))

    def send(stage, value):
        buf, me, peer = stages[stage]
        buf[me] = value
        for j in range(1, buf.shape[0]):
            stage_copy(stage, buf, me, peer, j).start()

    def receive(stage):
        buf = stages[stage][0]
        others = buf.at[pl.ds(1, buf.shape[0] - 1)]
        pltpu.make_async_copy(others, others, st_recv.at[stage]).wait()

    def total_of(buf, slots):
        values = [buf[s] for s in slots]
        while len(values) > 1:
            values = [a + b for a, b in zip(values[::2], values[1::2])]
        return values[0]

    for k in range(early_n + 2, rs_n):
        if k == early_n + 2:
            send(0, col_part[:, :early])
        elif k == early_n + 3:
            receive(0)
            send(1, total_of(x_buf, range(4)))
        elif k == early_n + 4:
            receive(1)
            send(2, total_of(y_buf, range(4)))
        step(k, k + AHEAD < rs_n)
        take(k - 2)
    receive(2)
    loads[3].wait()
    loads[4].wait()
    next_early = decay_rate * col_mom[:, :early] + (1.0 - decay_rate) * (total_of(d_buf, range(4)) / all_rows + tiny_value)
    new_cols[:, :early] = next_early
    inv_cols[:, :early] = jnp.broadcast_to(1.0 / next_early, (8, early))

    @pl.loop(0, strips)
    def _(r):
        down = pl.ds(pl.multiple_of(r * 8, 8), 8)
        parts = [jnp.zeros((8, LANES), jnp.float32) for _ in range(4)]
        for c in range(early // LANES):
            lanes = pl.ds(c * LANES, LANES)
            g = mine[down, lanes]
            parts[c % 4] = parts[c % 4] + g * g * inv_cols[:, lanes]
        w_part[down] = (parts[0] + parts[1]) + (parts[2] + parts[3])

    for k in range(rs_n - 2, rs_n):
        take(k)

    eye = lax.broadcasted_iota(jnp.int32, (rows, LANES), 0) == lax.broadcasted_iota(jnp.int32, (rows, LANES), 1)
    row_sums = jnp.sum(row_part[...], axis=1, keepdims=True)
    send(3, jnp.sum(jnp.where(eye, row_sums, 0.0), axis=0, keepdims=True))
    share = (decay_rate * col_mom[:, early:] + (1.0 - decay_rate) * tiny_value) / 64.0
    share = share + col_part[:, early:] * ((1.0 - decay_rate) / all_rows)
    receive(3)
    row_mean = total_of(r_buf, range(4)) / full_width + tiny_value
    next_rows = decay_rate * row_mom[...] + (1.0 - decay_rate) * row_mean
    new_rows[...] = next_rows
    rows_down = jnp.sum(jnp.where(eye, next_rows, 0.0), axis=1, keepdims=True)
    inv_rows[...] = jnp.broadcast_to(1.0 / rows_down, inv_rows.shape)

    weighted = []
    for c in range(early // LANES, width // LANES):
        lanes = pl.ds(c * LANES, LANES)
        parts = [jnp.zeros((8, LANES), jnp.float32) for _ in range(2)]
        for r in range(strips):
            down = pl.ds(8 * r, 8)
            g = mine[down, lanes]
            parts[r % 2] = parts[r % 2] + g * g * inv_rows[down]
        weighted.append(jnp.sum(parts[0] + parts[1], axis=0, keepdims=True))
    parts = [jnp.zeros((8, LANES), jnp.float32) for _ in range(2)]
    for r in range(strips):
        down = pl.ds(8 * r, 8)
        parts[r % 2] = parts[r % 2] + w_part[down] * inv_rows[down]
    rest = jnp.sum(parts[0] + parts[1], axis=0, keepdims=True)
    send(4, jnp.concatenate([share] + weighted + [rest, next_rows], axis=1))
    inv_cols[:, :early] = jnp.broadcast_to(lax.rsqrt(new_cols[:, :early]), (8, early))
    inv_rows[...] = jnp.sqrt(inv_rows[...])
    loads[5].wait()
    receive(4)
    send(5, total_of(f_buf, range(16)))
    receive(5)

    squares = jnp.zeros((1, LANES), jnp.float32)
    for c in range(4):
        both = total_of(g_buf, range(c, 16, 4))
        ratio = both[:, LATE:2 * LATE] / both[:, :LATE]
        squares = squares + both[:, 2 * LATE:2 * LATE + LANES]
        for k in range(LATE // LANES):
            squares = squares + ratio[:, k * LANES:(k + 1) * LANES]
        if c == 0:
            scale_mean = jnp.sum(both[:, 2 * LATE + LANES:], axis=(0, 1), keepdims=True) / all_rows
    update_sum = jnp.sum(squares, axis=(0, 1), keepdims=True) * scale_mean
    rms_update = jnp.sqrt(update_sum / (float(all_rows) * float(full_width)))
    rms_out[...] = rms_update
    factor = step_rate * jnp.sqrt(scale_mean) / jnp.maximum(1.0, rms_update)
    next_late = total_of(g_buf.at[:, :, :LATE], [col + 4 * d for d in range(4)])
    new_cols[:, early:] = next_late
    inv_cols[:, early:] = jnp.broadcast_to(lax.rsqrt(next_late), (8, LATE))
    inv_rows[...] = inv_rows[...] * factor

    ag_n = rows // AG_ROWS
    ag_half = ag_n // 2

    def ag_copy(way, k, passed, early=False):
        to = right if way == 0 else left
        at = pl.ds(pl.multiple_of(k * AG_ROWS, AG_ROWS), AG_ROWS)
        slot = (left if way == 0 else right) if passed else dp
        if early:
            sem = k if way == 0 else k - ag_half
        else:
            sem = ag_half
        return pltpu.make_async_remote_copy(
            src_ref=copies.at[slot, at], dst_ref=copies.at[slot, at], send_sem=ag_send.at[way, int(passed)],
            recv_sem=ag_recv.at[way, sem], device_id={"dp": to}, device_id_type=MESH)

    def give(k):
        base = pl.multiple_of(k * AG_ROWS, AG_ROWS)
        at = pl.ds(base, AG_ROWS)
        scale = inv_rows[at]
        for c in range(width // LANES):
            lanes = pl.ds(c * LANES, LANES)
            across = inv_cols[:, lanes]
            across = jnp.concatenate([across] * (AG_ROWS // 8), axis=0)
            w = mast[at, lanes] - mine[at, lanes] * scale * across
            new_master[at, lanes] = w
            copies[dp, at, lanes] = w.astype(jnp.bfloat16)

    @pl.loop(0, ag_half)
    def _(k):
        give(k)
        ag_copy(0, k, False, True).start()
        give(k + ag_half)
        ag_copy(1, k + ag_half, False, True).start()

    @pl.loop(0, ag_half)
    def _(k):
        ag_copy(0, k + ag_half, False).start()
        ag_copy(1, k, False).start()
        ag_copy(0, k, False, True).wait_recv()
        ag_copy(0, k, True).start()
        ag_copy(1, k + ag_half, False, True).wait_recv()
        ag_copy(1, k + ag_half, True).start()

    for way in (0, 1):
        for phase in (0, 1, 2):
            pltpu.make_async_copy(opp_l, opp_l, rs_send.at[way, phase]).wait()
    for stage, (buf, _, _) in enumerate(stages):
        others = buf.at[pl.ds(1, buf.shape[0] - 1)]
        pltpu.make_async_copy(others, others, st_send.at[stage]).wait()
    for way in (0, 1):
        pltpu.make_async_copy(copies.at[dp], copies.at[dp], ag_send.at[way, 0]).wait()
        passed = copies.at[far, pl.ds(0, half)]
        pltpu.make_async_copy(passed, passed, ag_send.at[way, 1]).wait()
        pltpu.make_async_copy(copies.at[far], copies.at[far], ag_recv.at[way, ag_half]).wait()


def write_out(*refs):
    sources, results, sem = refs[:5], refs[5:10], refs[10]
    pieces = [(sources[3].at[d], results[3].at[d]) for d in range(4)]
    half = sources[0].shape[0] // 2
    pieces += [(sources[0].at[pl.ds(h * half, half)], results[0].at[pl.ds(h * half, half)]) for h in range(2)]
    pieces += [(sources[i], results[i]) for i in (1, 2, 4)]
    moves = [pltpu.make_async_copy(a, b, sem.at[i]) for i, (a, b) in enumerate(pieces)]
    for move in moves:
        move.start()
    for move in moves:
        move.wait()


def local(grad_partials, master_weights, row_moment, col_moment):
    rows, width = master_weights.shape
    all_rows = rows * lax.axis_size("dp") * lax.axis_size("row")
    full_width = width * lax.axis_size("col")
    half = rows // 2
    rs_n, ag_n = width // CHUNK, rows // AG_ROWS
    early = width - LATE
    message = 2 * LATE + 2 * LANES
    f32 = jnp.float32
    hbm = pl.BlockSpec(memory_space=pltpu.HBM)
    vmem = pl.BlockSpec(memory_space=pltpu.VMEM)
    results = (
        jax.ShapeDtypeStruct((rows, width), f32),
        jax.ShapeDtypeStruct((1, rows), f32),
        jax.ShapeDtypeStruct((1, width), f32),
        jax.ShapeDtypeStruct((4, rows, width), jnp.bfloat16),
        jax.ShapeDtypeStruct((1, 1), f32),
    )
    held = pl.pallas_call(
        functools.partial(kernel, all_rows, full_width),
        out_shape=results,
        in_specs=[hbm, hbm, hbm, hbm],
        out_specs=(vmem,) * 5,
        scratch_shapes=[
            pltpu.VMEM((half, width), f32), pltpu.VMEM((half, width), f32),
            pltpu.VMEM((half, width), f32), pltpu.VMEM((half, width), f32),
            pltpu.VMEM((rows, width), f32), pltpu.VMEM((rows, width), f32),
            pltpu.VMEM((rows, width), f32), pltpu.VMEM((rows, width), f32),
            pltpu.VMEM((1, rows), f32), pltpu.VMEM((1, width), f32),
            pltpu.VMEM((rows, LANES), f32), pltpu.VMEM((rows, LANES), f32),
            pltpu.VMEM((1, width), f32), pltpu.VMEM((8, width), f32),
            pltpu.VMEM((rows, LANES), f32),
            pltpu.VMEM((4, 1, early), f32), pltpu.VMEM((4, 1, early), f32), pltpu.VMEM((4, 1, early), f32),
            pltpu.VMEM((4, 1, rows), f32),
            pltpu.VMEM((16, 1, message), f32), pltpu.VMEM((16, 1, message), f32),
            pltpu.SemaphoreType.DMA((6,)),
            pltpu.SemaphoreType.DMA((2, 3)), pltpu.SemaphoreType.DMA((2, 2, rs_n)),
            pltpu.SemaphoreType.DMA((6,)), pltpu.SemaphoreType.DMA((6,)),
            pltpu.SemaphoreType.DMA((2, 2)), pltpu.SemaphoreType.DMA((2, ag_n // 2 + 1)),
            pltpu.SemaphoreType.REGULAR((2,)),
        ],
        compiler_params=pltpu.CompilerParams(
            collective_id=0, has_side_effects=True, vmem_limit_bytes=40 * 1024 * 1024),
        cost_estimate=pl.CostEstimate(flops=10 * rows * width, bytes_accessed=40 * rows * width, transcendentals=0),
        name="adafactor",
    )(*[pltpu.with_memory_space_constraint(a, pltpu.HBM) for a in (grad_partials, master_weights, row_moment.reshape(1, rows), col_moment.reshape(1, width))])
    new_master, new_rows, new_cols, copies, rms = pl.pallas_call(
        write_out,
        out_shape=results,
        in_specs=[pl.BlockSpec(memory_space=pl.ANY)] * 5,
        out_specs=(hbm,) * 5,
        scratch_shapes=[pltpu.SemaphoreType.DMA((9,))],
        compiler_params=pltpu.CompilerParams(vmem_limit_bytes=1024 * 1024),
        cost_estimate=pl.CostEstimate(flops=0, bytes_accessed=24 * rows * width, transcendentals=0),
        name="write_out",
    )(*[pltpu.with_memory_space_constraint(a, pltpu.VMEM) for a in held])
    return (new_master, new_rows.reshape(rows), new_cols.reshape(width), copies, rms.reshape(()))


def solution(mesh):
    return jax.shard_map(
        local,
        mesh=mesh,
        in_specs=(P("dp", None, "row", "col"), P(("dp", "row"), "col"), P(("dp", "row")), P("col")),
        out_specs=(P(("dp", "row"), "col"), P(("dp", "row")), P("col"), P(None, "row", "col"), P()),
        check_vma=False,
    )
```

time: 727 us -> 240 us (0.33); the launches traced: 718 us -> 240 us
  blocking collectives: 456 us -> 0 us
  Pallas kernels: 0 us -> 239 us
  waiting for transfers between devices: 233 us -> 0 us
  between operations: 16.6 us -> 0.64 us
  other arithmetic: 7.76 us -> 0 us
    psum x3 -> x0, blocking collectives: 456 us -> none  [the longest x1 324 us: local(): col_totals, moment_sum = lax.psum((local_cols, rows_sum), ('dp', 'row'))]
    pallas_call x0 -> x2, Pallas kernels: none -> 239 us  [the longest x1 236 us: local(): pl.pallas_call(functools.partial(kernel, all_rows, full_width), out_shape...]
    reduce_scatter x1 -> x0, waiting for transfers between devices: 158 us -> none  [local(): lax.psum_scatter(local_grads, 'dp', scatter_dimension=0, tiled=True)]
    all_gather x1 -> x0, waiting for transfers between devices: 73.7 us -> none  [local(): lax.all_gather(new_weights.astype(jnp.bfloat16)[None], 'dp', axis=0, tile...]
  transfers between devices with their start and end apart: 2 -> 0, of which waited for: 2 -> 0; matrix products, arithmetic and copies ran while one was open for 0% -> 0% of each run, Pallas kernels for 0% -> 0%
where the time goes in v2:
time: 240 us
  Pallas kernels  239 us (100%)
    pallas_call x1, Pallas kernels, local(): pl.pallas_call(functools.partial(kernel, all_rows, full_width), out_shape...  236 us

profile of v2, /device:TPU:1, one launch (start us, length us, event | category | flops | bytes accessed | tf_op | source)
XLA Modules:
  0.0 239.8 jit_solution(1278263296807671832)
XLA Ops:
  0.6 235.7 %adafactor.1 = (f32[128,4096]{1,0:T(8,128)S(1)}, f32[1,128]{1,0:T(1,128)S(1)}, f32[1,4096]{1,0:T(1,128)S(1)}, bf16[4,128,4096]{2,1,0:T(8,128)(2,1)S(1)}, f32[1,1]{1,0:T(1,128)}) custom-call(f32[1,4,128,4096]{3,2,1,0:T(8,128)} %grads.1, f32[128,4096]{1,0:T(8,128)} %master.1, f32[1,128]{1,0:T(1,128)} %bitcast.6, f32[1,4096]{1,0:T(1,128)} %bitcast.5), custom_call_target="tpu_custom_call" | custom-call | flops 5242880 | bytes 20971520 | tf_op jit(solution)/shard_map/adafactor/pallas_call | solution.py:348
  236.4 3.4 %write_out.1 = (f32[128,4096]{1,0:T(8,128)}, f32[1,128]{1,0:T(1,128)}, f32[1,4096]{1,0:T(1,128)}, bf16[4,128,4096]{2,1,0:T(8,128)(2,1)}, f32[1,1]{1,0:T(1,128)}) custom-call(f32[128,4096]{1,0:T(8,128)S(1)} %get-tuple-element.15.refs_0_, f32[1,128]{1,0:T(1,128)S(1)} %get-tuple-element.16.refs_1_, f32[1,4096]{1,0:T(1,128)S(1)} %get-tuple-element.17.refs_2_, ...), custom_call_target="tpu_custom_call" | custom-call | bytes 12582912 | tf_op jit(solution)/shard_map/write_out/pallas_call | solution.py:376

commit v3 on v2

--- a/solution.py
+++ b/solution.py
@@ -14,7 +14,7 @@
 MESH = pl.DeviceIdType.MESH
 LANES = 128
 CHUNK = 256
-LATE = 1280
+LATE = 768
 AHEAD = 1
 AG_ROWS = 16
 
@@ -56,7 +56,8 @@
     def signal(sem, peer):
         pl.semaphore_signal(sem, inc=1, device_id=peer, device_id_type=MESH)
 
-    near = [d_peer(1), d_peer(3), x_peer(1), x_peer(3), y_peer(1), y_peer(3), c_peer(1), c_peer(2), c_peer(3)]
+    near = [d_peer(1), d_peer(3), x_peer(1), y_peer(1), c_peer(1)]
+    back = [x_peer(3), y_peer(3), c_peer(3)]
     barrier = pltpu.get_barrier_semaphore()
     for peer in near:
         signal(barrier, peer)
@@ -93,16 +94,15 @@
         rs_copy(0, 0, k).start()
         rs_copy(1, 0, k).start()
 
-    for peer in near:
+    for peer in back:
         signal(ready.at[0], peer)
     row_part[...] = jnp.zeros_like(row_part)
     loads[0].wait()
     loads[1].wait()
     loads[2].wait()
-    pl.semaphore_wait(ready.at[0], len(near))
-    for j in (1, 2, 3):
-        signal(ready.at[1], y_peer(j))
-        signal(ready.at[1], d_peer(j))
+    pl.semaphore_wait(ready.at[0], len(back))
+    for peer in back:
+        signal(ready.at[1], peer)
 
     def add_strips(add, opp, k):
         at = pl.ds(pl.multiple_of(k * CHUNK, CHUNK), CHUNK)
@@ -127,12 +127,14 @@
             row_part[down] = row_part[down] + across
         col_part[:, at] = jnp.sum(cols, axis=0, keepdims=True)
 
-    def step(k, more=True):
+    def issue(k, more=True):
         if more:
             rs_copy(0, 0, k + AHEAD).start()
             rs_copy(1, 0, k + AHEAD).start()
         rs_copy(0, 1, k).start()
         rs_copy(1, 1, k).start()
+
+    def pass_on(k):
         rs_copy(0, 0, k).wait_recv()
         add_strips(add_r, opp_l, k)
         rs_copy(0, 2, k).start()
@@ -140,15 +142,26 @@
         add_strips(add_l, opp_r, k)
         rs_copy(1, 2, k).start()
 
-    @pl.loop(0, early_n + 2)
+    @pl.loop(0, early_n + 1)
     def _(k):
-        step(k)
+        issue(k)
 
         @pl.when(k >= 2)
         def _():
             take(k - 2)
 
-    pl.semaphore_wait(ready.at[1], 6)
+        pass_on(k)
+
+        @pl.when(k == 4)
+        def _():
+            pl.semaphore_wait(ready.at[1], len(back))
+            for j in (1, 2, 3):
+                signal(ready.at[2], y_peer(j))
+                signal(ready.at[2], d_peer(j))
+
+        @pl.when(k == 8)
+        def _():
+            pl.semaphore_wait(ready.at[2], 6)
 
     def stage_copy(stage, buf, me, peer, j):
         return pltpu.make_async_remote_copy(
@@ -175,17 +188,17 @@
             values = [a + b for a, b in zip(values[::2], values[1::2])]
         return values[0]
 
-    for k in range(early_n + 2, rs_n):
+    for k in range(early_n + 1, rs_n):
         if k == early_n + 2:
-            send(0, col_part[:, :early])
-        elif k == early_n + 3:
             receive(0)
             send(1, total_of(x_buf, range(4)))
-        elif k == early_n + 4:
             receive(1)
             send(2, total_of(y_buf, range(4)))
-        step(k, k + AHEAD < rs_n)
+        issue(k, k + AHEAD < rs_n)
         take(k - 2)
+        if k == early_n + 1:
+            send(0, col_part[:, :early])
+        pass_on(k)
     receive(2)
     loads[3].wait()
     loads[4].wait()
@@ -366,7 +379,7 @@
             pltpu.SemaphoreType.DMA((2, 3)), pltpu.SemaphoreType.DMA((2, 2, rs_n)),
             pltpu.SemaphoreType.DMA((6,)), pltpu.SemaphoreType.DMA((6,)),
             pltpu.SemaphoreType.DMA((2, 2)), pltpu.SemaphoreType.DMA((2, ag_n // 2 + 1)),
-            pltpu.SemaphoreType.REGULAR((2,)),
+            pltpu.SemaphoreType.REGULAR((3,)),
         ],
         compiler_params=pltpu.CompilerParams(
             collective_id=0, has_side_effects=True, vmem_limit_bytes=40 * 1024 * 1024),

time: 240 us -> 238 us (level)
  no operation moved by 1% of the time
where the time goes in v3:
time: 238 us
  Pallas kernels  237 us (100%)
    pallas_call x1, Pallas kernels, local(): pl.pallas_call(functools.partial(kernel, all_rows, full_width), out_shape...  234 us

profile of v3, /device:TPU:1, one launch (start us, length us, event | category | flops | bytes accessed | tf_op | source)
XLA Modules:
  0.0 237.6 jit_solution(15602547742782765073)
XLA Ops:
  0.6 233.6 %adafactor.1 = (f32[128,4096]{1,0:T(8,128)S(1)}, f32[1,128]{1,0:T(1,128)S(1)}, f32[1,4096]{1,0:T(1,128)S(1)}, bf16[4,128,4096]{2,1,0:T(8,128)(2,1)S(1)}, f32[1,1]{1,0:T(1,128)}) custom-call(f32[1,4,128,4096]{3,2,1,0:T(8,128)} %grads.1, f32[128,4096]{1,0:T(8,128)} %master.1, f32[1,128]{1,0:T(1,128)} %bitcast.6, f32[1,4096]{1,0:T(1,128)} %bitcast.5), custom_call_target="tpu_custom_call" | custom-call | flops 5242880 | bytes 20971520 | tf_op jit(solution)/shard_map/adafactor/pallas_call | solution.py:361
  234.2 3.4 %write_out.1 = (f32[128,4096]{1,0:T(8,128)}, f32[1,128]{1,0:T(1,128)}, f32[1,4096]{1,0:T(1,128)}, bf16[4,128,4096]{2,1,0:T(8,128)(2,1)}, f32[1,1]{1,0:T(1,128)}) custom-call(f32[128,4096]{1,0:T(8,128)S(1)} %get-tuple-element.15.refs_0_, f32[1,128]{1,0:T(1,128)S(1)} %get-tuple-element.16.refs_1_, f32[1,4096]{1,0:T(1,128)S(1)} %get-tuple-element.17.refs_2_, ...), custom_call_target="tpu_custom_call" | custom-call | bytes 12582912 | tf_op jit(solution)/shard_map/write_out/pallas_call | solution.py:389

commit v4 on v3

--- a/solution.py
+++ b/solution.py
@@ -22,7 +22,7 @@
 def kernel(all_rows, full_width, grads, master, row_mom_hbm, col_mom_hbm,
            new_master, new_rows, new_cols, copies, rms_out,
            opp_l, opp_r, add_r, add_l, own_l, own_r, mine, mast, row_mom, col_mom,
-           row_part, w_part, col_part, inv_cols, inv_rows, x_buf, y_buf, d_buf, r_buf, f_buf, g_buf,
+           row_part, w_part, col_part, inv_cols, inv_rows, x_buf, y_buf, d_buf, r_buf, f_buf, g_buf, h_buf,
            load_sem, rs_send, rs_recv, st_send, st_recv, ag_send, ag_recv, ready):
     dp, row, col = lax.axis_index("dp"), lax.axis_index("row"), lax.axis_index("col")
     y, x = row // 4, row % 4
@@ -169,7 +169,7 @@
             recv_sem=st_recv.at[stage], device_id=peer(j), device_id_type=MESH)
 
     stages = ((x_buf, x, x_peer), (y_buf, y, y_peer), (d_buf, dp, d_peer), (r_buf, col, c_peer),
-              (f_buf, row, row_peer), (g_buf, dp * 4 + col, z_peer))
+              (f_buf, row, row_peer), (g_buf, dp, d_peer), (h_buf, col, c_peer))
 
     def send(stage, value):
         buf, me, peer = stages[stage]
@@ -199,6 +199,12 @@
         if k == early_n + 1:
             send(0, col_part[:, :early])
         pass_on(k)
+    for k in range(rs_n - 2, rs_n):
+        take(k)
+
+    eye = lax.broadcasted_iota(jnp.int32, (rows, LANES), 0) == lax.broadcasted_iota(jnp.int32, (rows, LANES), 1)
+    row_sums = jnp.sum(row_part[...], axis=1, keepdims=True)
+    send(3, jnp.sum(jnp.where(eye, row_sums, 0.0), axis=0, keepdims=True))
     receive(2)
     loads[3].wait()
     loads[4].wait()
@@ -216,12 +222,6 @@
             parts[c % 4] = parts[c % 4] + g * g * inv_cols[:, lanes]
         w_part[down] = (parts[0] + parts[1]) + (parts[2] + parts[3])
 
-    for k in range(rs_n - 2, rs_n):
-        take(k)
-
-    eye = lax.broadcasted_iota(jnp.int32, (rows, LANES), 0) == lax.broadcasted_iota(jnp.int32, (rows, LANES), 1)
-    row_sums = jnp.sum(row_part[...], axis=1, keepdims=True)
-    send(3, jnp.sum(jnp.where(eye, row_sums, 0.0), axis=0, keepdims=True))
     share = (decay_rate * col_mom[:, early:] + (1.0 - decay_rate) * tiny_value) / 64.0
     share = share + col_part[:, early:] * ((1.0 - decay_rate) / all_rows)
     receive(3)
@@ -252,23 +252,22 @@
     receive(4)
     send(5, total_of(f_buf, range(16)))
     receive(5)
-
-    squares = jnp.zeros((1, LANES), jnp.float32)
-    for c in range(4):
-        both = total_of(g_buf, range(c, 16, 4))
-        ratio = both[:, LATE:2 * LATE] / both[:, :LATE]
-        squares = squares + both[:, 2 * LATE:2 * LATE + LANES]
-        for k in range(LATE // LANES):
-            squares = squares + ratio[:, k * LANES:(k + 1) * LANES]
-        if c == 0:
-            scale_mean = jnp.sum(both[:, 2 * LATE + LANES:], axis=(0, 1), keepdims=True) / all_rows
+    both = total_of(g_buf, range(4))
+    next_late = both[:, :LATE]
+    ratio = both[:, LATE:2 * LATE] / next_late
+    squares = both[:, 2 * LATE:2 * LATE + LANES]
+    for c in range(LATE // LANES):
+        squares = squares + ratio[:, c * LANES:(c + 1) * LANES]
+    send(6, squares)
+    scale_mean = jnp.sum(both[:, 2 * LATE + LANES:], axis=(0, 1), keepdims=True) / all_rows
+    new_cols[:, early:] = next_late
+    inv_cols[:, early:] = jnp.broadcast_to(lax.rsqrt(next_late), (8, LATE))
+    receive(6)
+    squares = total_of(h_buf, range(4))
     update_sum = jnp.sum(squares, axis=(0, 1), keepdims=True) * scale_mean
     rms_update = jnp.sqrt(update_sum / (float(all_rows) * float(full_width)))
     rms_out[...] = rms_update
     factor = step_rate * jnp.sqrt(scale_mean) / jnp.maximum(1.0, rms_update)
-    next_late = total_of(g_buf.at[:, :, :LATE], [col + 4 * d for d in range(4)])
-    new_cols[:, early:] = next_late
-    inv_cols[:, early:] = jnp.broadcast_to(lax.rsqrt(next_late), (8, LATE))
     inv_rows[...] = inv_rows[...] * factor
 
     ag_n = rows // AG_ROWS
@@ -374,10 +373,10 @@
             pltpu.VMEM((rows, LANES), f32),
             pltpu.VMEM((4, 1, early), f32), pltpu.VMEM((4, 1, early), f32), pltpu.VMEM((4, 1, early), f32),
             pltpu.VMEM((4, 1, rows), f32),
-            pltpu.VMEM((16, 1, message), f32), pltpu.VMEM((16, 1, message), f32),
+            pltpu.VMEM((16, 1, message), f32), pltpu.VMEM((4, 1, message), f32), pltpu.VMEM((4, 1, LANES), f32),
             pltpu.SemaphoreType.DMA((6,)),
             pltpu.SemaphoreType.DMA((2, 3)), pltpu.SemaphoreType.DMA((2, 2, rs_n)),
-            pltpu.SemaphoreType.DMA((6,)), pltpu.SemaphoreType.DMA((6,)),
+            pltpu.SemaphoreType.DMA((7,)), pltpu.SemaphoreType.DMA((7,)),
             pltpu.SemaphoreType.DMA((2, 2)), pltpu.SemaphoreType.DMA((2, ag_n // 2 + 1)),
             pltpu.SemaphoreType.REGULAR((3,)),
         ],

time: 238 us -> 237 us (level)
  the two profiles are of different devices: /device:TPU:1 before, /device:TPU:33 now
where the time goes in v4:
time: 237 us
  Pallas kernels  236 us (100%)
    pallas_call x1, Pallas kernels, local(): pl.pallas_call(functools.partial(kernel, all_rows, full_width), out_shape...  233 us

profile of v4, /device:TPU:33, one launch (start us, length us, event | category | flops | bytes accessed | tf_op | source)
XLA Modules:
  0.0 236.9 jit_solution(15940773655200267516)
XLA Ops:
  0.6 232.8 %adafactor.1 = (f32[128,4096]{1,0:T(8,128)S(1)}, f32[1,128]{1,0:T(1,128)S(1)}, f32[1,4096]{1,0:T(1,128)S(1)}, bf16[4,128,4096]{2,1,0:T(8,128)(2,1)S(1)}, f32[1,1]{1,0:T(1,128)}) custom-call(f32[1,4,128,4096]{3,2,1,0:T(8,128)} %grads.1, f32[128,4096]{1,0:T(8,128)} %master.1, f32[1,128]{1,0:T(1,128)} %bitcast.6, f32[1,4096]{1,0:T(1,128)} %bitcast.5), custom_call_target="tpu_custom_call" | custom-call | flops 5242880 | bytes 20971520 | tf_op jit(solution)/shard_map/adafactor/pallas_call | solution.py:360
  233.5 3.4 %write_out.1 = (f32[128,4096]{1,0:T(8,128)}, f32[1,128]{1,0:T(1,128)}, f32[1,4096]{1,0:T(1,128)}, bf16[4,128,4096]{2,1,0:T(8,128)(2,1)}, f32[1,1]{1,0:T(1,128)}) custom-call(f32[128,4096]{1,0:T(8,128)S(1)} %get-tuple-element.15.refs_0_, f32[1,128]{1,0:T(1,128)S(1)} %get-tuple-element.16.refs_1_, f32[1,4096]{1,0:T(1,128)S(1)} %get-tuple-element.17.refs_2_, ...), custom_call_target="tpu_custom_call" | custom-call | bytes 12582912 | tf_op jit(solution)/shard_map/write_out/pallas_call | solution.py:388

commit v5 on v4

--- a/solution.py
+++ b/solution.py
@@ -306,12 +306,12 @@
 
     @pl.loop(0, ag_half)
     def _(k):
-        ag_copy(0, k + ag_half, False).start()
-        ag_copy(1, k, False).start()
         ag_copy(0, k, False, True).wait_recv()
         ag_copy(0, k, True).start()
         ag_copy(1, k + ag_half, False, True).wait_recv()
         ag_copy(1, k + ag_half, True).start()
+        ag_copy(0, k + ag_half, False).start()
+        ag_copy(1, k, False).start()
 
     for way in (0, 1):
         for phase in (0, 1, 2):

time: 237 us -> 237 us (level)
  no operation moved by 1% of the time
where the time goes in v5:
time: 237 us
  Pallas kernels  236 us (100%)
    pallas_call x1, Pallas kernels, local(): pl.pallas_call(functools.partial(kernel, all_rows, full_width), out_shape...  233 us

profile of v5, /device:TPU:33, one launch (start us, length us, event | category | flops | bytes accessed | tf_op | source)
XLA Modules:
  0.0 236.9 jit_solution(8554346048233453124)
XLA Ops:
  0.6 232.8 %adafactor.1 = (f32[128,4096]{1,0:T(8,128)S(1)}, f32[1,128]{1,0:T(1,128)S(1)}, f32[1,4096]{1,0:T(1,128)S(1)}, bf16[4,128,4096]{2,1,0:T(8,128)(2,1)S(1)}, f32[1,1]{1,0:T(1,128)}) custom-call(f32[1,4,128,4096]{3,2,1,0:T(8,128)} %grads.1, f32[128,4096]{1,0:T(8,128)} %master.1, f32[1,128]{1,0:T(1,128)} %bitcast.6, f32[1,4096]{1,0:T(1,128)} %bitcast.5), custom_call_target="tpu_custom_call" | custom-call | flops 5242880 | bytes 20971520 | tf_op jit(solution)/shard_map/adafactor/pallas_call | solution.py:360
  233.5 3.4 %write_out.1 = (f32[128,4096]{1,0:T(8,128)}, f32[1,128]{1,0:T(1,128)}, f32[1,4096]{1,0:T(1,128)}, bf16[4,128,4096]{2,1,0:T(8,128)(2,1)}, f32[1,1]{1,0:T(1,128)}) custom-call(f32[128,4096]{1,0:T(8,128)S(1)} %get-tuple-element.15.refs_0_, f32[1,128]{1,0:T(1,128)S(1)} %get-tuple-element.16.refs_1_, f32[1,4096]{1,0:T(1,128)S(1)} %get-tuple-element.17.refs_2_, ...), custom_call_target="tpu_custom_call" | custom-call | bytes 12582912 | tf_op jit(solution)/shard_map/write_out/pallas_call | solution.py:388
